TPU v7x, 32 devices: a whole 2x2x4 slice. The times are simulated.
32 devices in a mesh: dp: 16 (over z, y, core), pipe: 2 (over x).
Axes of the slice: x: 2, y: 2, z: 4, core: 2. Of those that a mesh axis runs over, the one named last changes fastest.
Arguments:
- clean: bfloat16 [64, 128, 320], P('dp'), may hold values from -20 to 20
- noise: bfloat16 [64, 128, 320], P('dp'), may hold values from -6 to 6
- timesteps: int32 [64], P('dp'), may hold values from 0 to 999
- enc_in: bfloat16 [2, 320, 1280], P('pipe'), may hold values from -0.3125 to 0.3125
- enc_out: bfloat16 [2, 1280, 320], P('pipe'), may hold values from -0.15625 to 0.15625
- enc_gain: float32 [2, 320], P('pipe'), may hold values from 0.5 to 1.5
- time_gain: float32 [2, 320], P('pipe'), may hold values from -3 to 3
- dec_w: bfloat16 [2, 640, 320], P('pipe'), may hold values from -0.25 to 0.25
- dec_gain: float32 [2, 640], P('pipe'), may hold values from 0.5 to 1.5
Outputs:
- loss: float32 [], replicated
- grad_enc_in: bfloat16 [2, 320, 1280], P('pipe')
- grad_enc_out: bfloat16 [2, 1280, 320], P('pipe')
- grad_enc_gain: float32 [2, 320], P('pipe')
- grad_dec_w: bfloat16 [2, 640, 320], P('pipe')
- grad_dec_gain: float32 [2, 640], P('pipe')
All inputs are finite; a program needn't handle non-finite values.
Results may differ from a plain program's by a relative error of at most 0.004.
Values may be sent and summed in bfloat16 or wider, within the bound.
No kernel may reach another device: no remote copies, remote signals or barrier semaphores. Data moves between devices by JAX's collectives and lax.ppermute only.
A program may use at most 64 MiB of HBM per device.

v0:
```python
import math
import jax
import jax.numpy as jnp
from jax import lax
from jax.sharding import PartitionSpec as P

TSTEPS = 1000
EPS = 1e-06
GELU_SCALE = math.sqrt(2.0 / math.pi)
CUBIC = 0.044715


def from_behind(shard, axis, by):
    peers = lax.axis_size(axis)
    pairs = [(i, i + by) for i in range(peers) if 0 <= i + by < peers]
    return lax.ppermute(shard, axis, pairs)


def left_dot(matrix_a, matrix_b):
    return lax.dot_general(
        matrix_a, matrix_b, (((0,), (0,)), ((), ())), preferred_element_type=jnp.float32
    )


def right_dot(matrix_a, matrix_b):
    return lax.dot_general(
        matrix_a, matrix_b, (((1,), (1,)), ((), ())), preferred_element_type=jnp.float32
    )


def plan(step_ids):
    angles = 0.5 * math.pi * (step_ids.astype(jnp.float32) + 0.5) / TSTEPS
    return (jnp.cos(angles), jnp.sin(angles))


def features(step_ids, channels):
    half_width = channels // 2
    frequency = jnp.exp(-math.log(10000.0) * jnp.arange(half_width, dtype=jnp.float32) / half_width)
    angles = step_ids.astype(jnp.float32)[:, None] * frequency[None, :]
    return jnp.concatenate([jnp.sin(angles), jnp.cos(angles)], axis=1)


def normalize(inputs):
    values = inputs.astype(jnp.float32)
    inverse = lax.rsqrt(jnp.mean(values * values, axis=-1, keepdims=True) + EPS)
    return (values * inverse, inverse)


def norm_back(grad_unit, unit_rows, inverse):
    return (
        grad_unit - unit_rows * jnp.mean(grad_unit * unit_rows, axis=-1, keepdims=True)
    ) * inverse


def gelu_value(pre_act):
    inner = GELU_SCALE * (pre_act + CUBIC * pre_act * pre_act * pre_act)
    return 0.5 * pre_act * (1.0 + jnp.tanh(inner))


def gelu_slope(pre_act):
    tanh_val = jnp.tanh(GELU_SCALE * (pre_act + CUBIC * pre_act * pre_act * pre_act))
    return 0.5 * (1.0 + tanh_val) + 0.5 * pre_act * (1.0 - tanh_val * tanh_val) * GELU_SCALE * (
        1.0 + 3.0 * CUBIC * pre_act * pre_act
    )


def encode_parts(inputs, embedding, norm_gain, weight_in):
    unit_rows, inverse = normalize(inputs)
    normed = (unit_rows * norm_gain + embedding).astype(jnp.bfloat16)
    pre_act = jnp.dot(normed, weight_in, preferred_element_type=jnp.float32)
    hidden = gelu_value(pre_act).astype(jnp.bfloat16)
    return (unit_rows, inverse, normed, pre_act, hidden)


def encode(inputs, embedding, norm_gain, weight_in, weight_out):
    hidden = encode_parts(inputs, embedding, norm_gain, weight_in)[4]
    return (
        inputs.astype(jnp.float32) + jnp.dot(hidden, weight_out, preferred_element_type=jnp.float32)
    ).astype(jnp.bfloat16)


def encode_back(inputs, embedding, norm_gain, weight_in, weight_out, grad_y):
    unit_rows, inverse, normed, pre_act, hidden = encode_parts(
        inputs, embedding, norm_gain, weight_in
    )
    grad_out = left_dot(hidden, grad_y)
    grad_hidden = right_dot(grad_y, weight_out)
    grad_pre = (grad_hidden * gelu_slope(pre_act)).astype(jnp.bfloat16)
    grad_in = left_dot(normed, grad_pre)
    grad_normed = right_dot(grad_pre, weight_in)
    grad_gain = jnp.sum(grad_normed * unit_rows, axis=0)
    grad_x = grad_y.astype(jnp.float32) + norm_back(grad_normed * norm_gain, unit_rows, inverse)
    return (grad_x, grad_in, grad_out, grad_gain)


def decode_parts(inputs, skip_rows, norm_gain):
    channels = inputs.shape[-1]
    unit_x, inv_x = normalize(inputs)
    unit_s, inv_s = normalize(skip_rows)
    joined = jnp.concatenate(
        [unit_x * norm_gain[:channels], unit_s * norm_gain[channels:]], axis=-1
    ).astype(jnp.bfloat16)
    return (unit_x, inv_x, unit_s, inv_s, joined)


def decode(inputs, skip_rows, norm_gain, weight):
    joined = decode_parts(inputs, skip_rows, norm_gain)[4]
    return (
        inputs.astype(jnp.float32) + jnp.dot(joined, weight, preferred_element_type=jnp.float32)
    ).astype(jnp.bfloat16)


def decode_back(inputs, skip_rows, norm_gain, weight, grad_y):
    channels = inputs.shape[-1]
    unit_x, inv_x, unit_s, inv_s, joined = decode_parts(inputs, skip_rows, norm_gain)
    grad_weight = left_dot(joined, grad_y)
    grad_joined = right_dot(grad_y, weight)
    grad_gain = jnp.sum(grad_joined * jnp.concatenate([unit_x, unit_s], axis=-1), axis=0)
    scaled = grad_joined * norm_gain
    grad_x = grad_y.astype(jnp.float32) + norm_back(scaled[:, :channels], unit_x, inv_x)
    grad_skip = norm_back(scaled[:, channels:], unit_s, inv_s)
    return (grad_x, grad_skip, grad_weight, grad_gain)


def take_slot(buffer, slot_index):
    return lax.dynamic_index_in_dim(buffer, slot_index, 0, keepdims=False)


def put_slot(buffer, slot_index, value, is_valid):
    previous = take_slot(buffer, slot_index)
    return lax.dynamic_update_index_in_dim(
        buffer, jnp.where(is_valid, value, previous), slot_index, 0
    )


def body(clean, noise, timesteps, enc_in, enc_out, enc_gain, time_gain, dec_w, dec_gain):
    levels = lax.axis_size("pipe")
    section_index = lax.axis_index("pipe")
    batches, row_count, channels = clean.shape
    hidden_units = enc_in.shape[2]
    total_rows = batches * lax.axis_size("dp") * row_count
    weight_in = enc_in[0]
    weight_out = enc_out[0]
    e_gain = enc_gain[0]
    d_weight = dec_w[0]
    d_gain = dec_gain[0]
    keep_rate, spread = plan(timesteps)
    keep_full = keep_rate[:, None, None]
    spread_full = spread[:, None, None]
    clean_f = clean.astype(jnp.float32)
    noise_f = noise.astype(jnp.float32)
    start_input = (keep_full * clean_f + spread_full * noise_f).astype(jnp.bfloat16)
    target = keep_full * noise_f - spread_full * clean_f
    time_embed = time_gain[0][None, :] * features(timesteps, channels)
    is_first = section_index == 0
    is_last = section_index == levels - 1
    act_zero = jnp.zeros((row_count, channels), jnp.bfloat16)
    grad_zero = jnp.zeros((row_count, channels), jnp.float32)
    act_buffer = jnp.zeros((batches, row_count, channels), jnp.bfloat16)

    def slot_of(micro):
        is_valid = (micro >= 0) & (micro < batches)
        return (is_valid, jnp.clip(micro, 0, batches - 1))

    def forward_tick(tick, loop_state, offset, run_up, run_down):
        recv_up, recv_down, enc_keep, dec_keep, top_rows, pred_rows = loop_state
        if run_up:
            is_valid, slot_index = slot_of(tick - section_index)
            block_in = jnp.where(is_first, take_slot(start_input, slot_index), recv_up)
            embedding = take_slot(time_embed, slot_index)[None, :]
            block_out = lax.cond(
                is_valid,
                lambda: encode(block_in, embedding, e_gain, weight_in, weight_out),
                lambda: act_zero,
            )
            enc_keep = put_slot(enc_keep, slot_index, block_in, is_valid)
            top_rows = put_slot(top_rows, slot_index, block_out, is_valid & is_last)
            recv_up = from_behind(block_out, "pipe", 1)
        if run_down:
            is_valid, slot_index = slot_of(tick - offset + section_index)
            block_in = jnp.where(is_last, take_slot(top_rows, slot_index), recv_down)
            skip_rows = take_slot(enc_keep, slot_index)
            block_out = lax.cond(
                is_valid, lambda: decode(block_in, skip_rows, d_gain, d_weight), lambda: act_zero
            )
            dec_keep = put_slot(dec_keep, slot_index, block_in, is_valid)
            pred_rows = put_slot(pred_rows, slot_index, block_out, is_valid & is_first)
            recv_down = from_behind(block_out, "pipe", -1)
        return (recv_up, recv_down, enc_keep, dec_keep, top_rows, pred_rows)

    loop_state = (act_zero, act_zero, act_buffer, act_buffer, act_buffer, act_buffer)
    loop_state = lax.fori_loop(
        0,
        batches + levels - 1,
        lambda tick, state: forward_tick(tick, state, 0, True, False),
        loop_state,
    )
    loop_state = lax.fori_loop(
        0,
        batches + levels - 1,
        lambda tick, state: forward_tick(tick, state, levels - 1, False, True),
        loop_state,
    )
    enc_keep = loop_state[2]
    dec_keep = loop_state[3]
    pred_rows = loop_state[5]
    residual = pred_rows.astype(jnp.float32) - target
    local_sum = jnp.where(is_first, jnp.sum(residual * residual), jnp.float32(0.0))
    loss_value = lax.psum(local_sum, ("dp", "pipe")) / (total_rows * channels)
    grad_seed = (residual / math.sqrt(total_rows)).astype(jnp.bfloat16)

    def backward_tick(tick, loop_state, offset, run_up, run_down):
        recv_up, recv_down, skip_grads, top_grads, dec_sums, enc_sums = loop_state
        if run_up:
            is_valid, slot_index = slot_of(tick - section_index)
            grad_y = jnp.where(is_first, take_slot(grad_seed, slot_index), recv_up)
            block_x = take_slot(dec_keep, slot_index)
            skip_rows = take_slot(enc_keep, slot_index)
            grad_x, grad_skip, grad_weight, grad_gain = lax.cond(
                is_valid,
                lambda: decode_back(block_x, skip_rows, d_gain, d_weight, grad_y),
                lambda: (
                    grad_zero,
                    grad_zero,
                    jnp.zeros((2 * channels, channels), jnp.float32),
                    jnp.zeros((2 * channels,), jnp.float32),
                ),
            )
            dec_sums = (dec_sums[0] + grad_weight, dec_sums[1] + grad_gain)
            grad_sent = grad_x.astype(jnp.bfloat16)
            skip_grads = put_slot(skip_grads, slot_index, grad_skip, is_valid)
            top_grads = put_slot(top_grads, slot_index, grad_sent, is_valid & is_last)
            recv_up = from_behind(grad_sent, "pipe", 1)
        if run_down:
            is_valid, slot_index = slot_of(tick - offset + section_index)
            grad_y = jnp.where(is_last, take_slot(top_grads, slot_index), recv_down)
            block_x = take_slot(enc_keep, slot_index)
            embedding = take_slot(time_embed, slot_index)[None, :]
            grad_x, grad_in, grad_out, grad_gain = lax.cond(
                is_valid,
                lambda: encode_back(block_x, embedding, e_gain, weight_in, weight_out, grad_y),
                lambda: (
                    grad_zero,
                    jnp.zeros((channels, hidden_units), jnp.float32),
                    jnp.zeros((hidden_units, channels), jnp.float32),
                    jnp.zeros((channels,), jnp.float32),
                ),
            )
            enc_sums = (enc_sums[0] + grad_in, enc_sums[1] + grad_out, enc_sums[2] + grad_gain)
            grad_sent = (grad_x + take_slot(skip_grads, slot_index)).astype(jnp.bfloat16)
            recv_down = from_behind(grad_sent, "pipe", -1)
        return (recv_up, recv_down, skip_grads, top_grads, dec_sums, enc_sums)

    dec_start = (
        jnp.zeros((2 * channels, channels), jnp.float32),
        jnp.zeros((2 * channels,), jnp.float32),
    )
    enc_start = (
        jnp.zeros((channels, hidden_units), jnp.float32),
        jnp.zeros((hidden_units, channels), jnp.float32),
        jnp.zeros((channels,), jnp.float32),
    )
    loop_state = (
        act_zero,
        act_zero,
        jnp.zeros((batches, row_count, channels), jnp.float32),
        act_buffer,
        dec_start,
        enc_start,
    )
    dec_done = None
    loop_state = lax.fori_loop(
        0,
        batches + levels - 1,
        lambda tick, state: backward_tick(tick, state, 0, True, False),
        loop_state,
    )
    loop_state = lax.fori_loop(
        0,
        batches + levels - 1,
        lambda tick, state: backward_tick(tick, state, levels - 1, False, True),
        loop_state,
    )
    dec_sums = loop_state[4]
    enc_sums = loop_state[5]
    summed = lax.psum((enc_sums[0], enc_sums[1], enc_sums[2], dec_sums[0], dec_sums[1]), "dp")
    enc_done = (summed[0], summed[1], summed[2])
    dec_done = (summed[3], summed[4])
    return (
        loss_value,
        enc_done[0].astype(jnp.bfloat16)[None],
        enc_done[1].astype(jnp.bfloat16)[None],
        enc_done[2][None],
        dec_done[0].astype(jnp.bfloat16)[None],
        dec_done[1][None],
    )


def solution(mesh):
    in_specs = (
        P("dp", None, None),
        P("dp", None, None),
        P("dp"),
        P("pipe", None, None),
        P("pipe", None, None),
        P("pipe", None),
        P("pipe", None),
        P("pipe", None, None),
        P("pipe", None),
    )
    out_specs = (
        P(),
        P("pipe", None, None),
        P("pipe", None, None),
        P("pipe", None),
        P("pipe", None, None),
        P("pipe", None),
    )
    return jax.shard_map(body, mesh=mesh, in_specs=in_specs, out_specs=out_specs, check_vma=False)
```

profile of v0, /device:TPU:19, one launch (start us, length us, event | category | flops | bytes accessed | tf_op | source)
XLA Modules:
  0.0 368.0 jit_solution(145540141024967541)
XLA Ops:
  7.3 2.2 copy.17
  9.7 37.5 %while.80 = (s32[]{:T(128)}, bf16[128,320]{0,1:T(8,128)(2,1)S(1)}, bf16[4,128,320]{1,2,0:T(8,128)(2,1)S(1)}, bf16[4,128,320]{1,2,0:T(8,128)(2,1)S(1)}, s32[]{:T(...) while((s32[]{:T(128)}, bf16[128,320]{0,1:T(8,128)(2,1)S(1)}, ...), condition=%wide.region_4.5_spmd, body=%wide.region_0.4_spmd.sunk | while | flops 211763328 | bytes 3204945 | solution.py:192
  9.8 1.3 collective-permute-start
  11.2 4.8 %collective-permute-done = bf16[128,320]{0,1:T(8,128)(2,1)S(1)} collective-permute-done((bf16[128,320]{0,1:T(8,128)(2,1)S(1)}, bf16[128,320]{0,1:T(8,128)(2,1)S(1)}, u32[]{:S(2)}, u32[]{:S(2)}) %collective-permute-start) | collective-permute-done | bytes 81952 | tf_op jit(solution)/shard_map/while/body/eval_jaxpr/ppermute | solution.py:16
  16.1 2.5 conditional.10
  16.2 2.4 fusion.11
  18.6 1.3 collective-permute-start
  20.0 3.8 %collective-permute-done = bf16[128,320]{0,1:T(8,128)(2,1)S(1)} collective-permute-done((bf16[128,320]{0,1:T(8,128)(2,1)S(1)}, bf16[128,320]{0,1:T(8,128)(2,1)S(1)}, u32[]{:S(2)}, u32[]{:S(2)}) %collective-permute-start) | collective-permute-done | bytes 81952 | tf_op jit(solution)/shard_map/while/body/eval_jaxpr/ppermute | solution.py:16
  23.9 2.5 conditional.10
  24.0 2.4 fusion.11
  27.8 3.8 %collective-permute-done = bf16[128,320]{0,1:T(8,128)(2,1)S(1)} collective-permute-done((bf16[128,320]{0,1:T(8,128)(2,1)S(1)}, bf16[128,320]{0,1:T(8,128)(2,1)S(1)}, u32[]{:S(2)}, u32[]{:S(2)}) %collective-permute-start) | collective-permute-done | bytes 81952 | tf_op jit(solution)/shard_map/while/body/eval_jaxpr/ppermute | solution.py:16
  31.7 2.5 conditional.10
  31.8 2.4 fusion.11
  35.6 3.8 %collective-permute-done = bf16[128,320]{0,1:T(8,128)(2,1)S(1)} collective-permute-done((bf16[128,320]{0,1:T(8,128)(2,1)S(1)}, bf16[128,320]{0,1:T(8,128)(2,1)S(1)}, u32[]{:S(2)}, u32[]{:S(2)}) %collective-permute-start) | collective-permute-done | bytes 81952 | tf_op jit(solution)/shard_map/while/body/eval_jaxpr/ppermute | solution.py:16
  39.5 2.5 conditional.10
  39.6 2.4 fusion.11
  43.4 3.8 %collective-permute-done = bf16[128,320]{0,1:T(8,128)(2,1)S(1)} collective-permute-done((bf16[128,320]{0,1:T(8,128)(2,1)S(1)}, bf16[128,320]{0,1:T(8,128)(2,1)S(1)}, u32[]{:S(2)}, u32[]{:S(2)}) %collective-permute-start) | collective-permute-done | bytes 81952 | tf_op jit(solution)/shard_map/while/body/eval_jaxpr/ppermute | solution.py:16
  47.3 29.2 %while.81 = (s32[]{:T(128)}, bf16[128,320]{0,1:T(8,128)(2,1)S(1)}, bf16[4,128,320]{1,2,0:T(8,128)(2,1)S(1)}, bf16[4,128,320]{1,2,0:T(8,128)(2,1)S(1)}, s32[]{:T(...) while((s32[]{:T(128)}, bf16[128,320]{0,1:T(8,128)(2,1)S(1)}, ...), condition=%wide.region_10.11_spmd, body=%wide.region_5.10_spmd.sunk | while | flops 53575944 | bytes 2551637 | solution.py:198
  48.2 1.3 collective-permute-start.1
  49.6 1.4 collective-permute-done.1
  51.8 3.7 %collective-permute-start.1 = (bf16[128,320]{0,1:T(8,128)(2,1)S(1)}, bf16[128,320]{0,1:T(8,128)(2,1)S(1)}, u32[]{:S(2)}, u32[]{:S(2)}) collective-permute-start(bf16[128,320]{0,1:T(8,128)(2,1)S(1)} %get-tuple-element.2173), channel_id=1, source_target_pairs={{1,0},{3,2},{5,4},{7,6},{9,8},{11,10},{13,12},{15,14},{17,16},{19,... | collective-permute-start | bytes 245768 | tf_op jit(solution)/shard_map/while/body/eval_jaxpr/ppermute | solution.py:16
  55.6 2.2 collective-permute-done.1
  58.6 4.1 %collective-permute-start.1 = (bf16[128,320]{0,1:T(8,128)(2,1)S(1)}, bf16[128,320]{0,1:T(8,128)(2,1)S(1)}, u32[]{:S(2)}, u32[]{:S(2)}) collective-permute-start(bf16[128,320]{0,1:T(8,128)(2,1)S(1)} %get-tuple-element.2173), channel_id=1, source_target_pairs={{1,0},{3,2},{5,4},{7,6},{9,8},{11,10},{13,12},{15,14},{17,16},{19,... | collective-permute-start | bytes 245768 | tf_op jit(solution)/shard_map/while/body/eval_jaxpr/ppermute | solution.py:16
  62.8 1.4 collective-permute-done.1
  65.0 4.0 %collective-permute-start.1 = (bf16[128,320]{0,1:T(8,128)(2,1)S(1)}, bf16[128,320]{0,1:T(8,128)(2,1)S(1)}, u32[]{:S(2)}, u32[]{:S(2)}) collective-permute-start(bf16[128,320]{0,1:T(8,128)(2,1)S(1)} %get-tuple-element.2173), channel_id=1, source_target_pairs={{1,0},{3,2},{5,4},{7,6},{9,8},{11,10},{13,12},{15,14},{17,16},{19,... | collective-permute-start | bytes 245768 | tf_op jit(solution)/shard_map/while/body/eval_jaxpr/ppermute | solution.py:16
  69.1 1.4 collective-permute-done.1
  70.6 4.4 %collective-permute-start.1 = (bf16[128,320]{0,1:T(8,128)(2,1)S(1)}, bf16[128,320]{0,1:T(8,128)(2,1)S(1)}, u32[]{:S(2)}, u32[]{:S(2)}) collective-permute-start(bf16[128,320]{0,1:T(8,128)(2,1)S(1)} %get-tuple-element.2173), channel_id=1, source_target_pairs={{1,0},{3,2},{5,4},{7,6},{9,8},{11,10},{13,12},{15,14},{17,16},{19,... | collective-permute-start | bytes 245768 | tf_op jit(solution)/shard_map/while/body/eval_jaxpr/ppermute | solution.py:16
  75.1 1.4 collective-permute-done.1
  78.5 1.9 copy.24
  80.4 2.7 multiply_convert_fusion.4
  83.8 51.1 %psum.42 = f32[]{:T(128)} all-reduce(f32[]{:T(128)S(6)} %select_n.216), channel_id=1, replica_groups=mesh['dp'=16,'pipe'=2] {'dp','pipe'}, use_global_device_ids=true, to_apply=%region_12.13 | all-reduce | flops 1 | bytes 8 | tf_op jit(solution)/shard_map/psum | solution.py:209
  138.1 49.6 %while.82 = (s32[]{:T(128)}, bf16[128,320]{1,0:T(8,128)(2,1)S(1)}, f32[4,128,320]{1,2,0:T(8,128)}, bf16[4,128,320]{1,2,0:T(8,128)(2,1)}, f32[640,320]{0,1:T(8,12...) while((s32[]{:T(128)}, bf16[128,320]{1,0:T(8,128)(2,1)S(1)}, ...), condition=%wide.region_21.22_spmd.clone, body=%wide.region_13.21_spmd.clone.sunk | while | flops 107316104 | bytes 10603944 | solution.py:272
  143.5 2.4 collective-permute-done.2
  145.9 5.1 %conditional.12 = (f32[128,320]{1,0:T(8,128)S(1)}, f32[640,320]{0,1:T(8,128)S(1)}, f32[640]{0:T(1024)S(1)}, bf16[128,320]{1,0:T(8,128)(2,1)S(1)}) conditional(s32[]{:T(128)} %convert_element_type.275, () %tuple.212, (pred[]{:T(512)}, bf16[4,128,320]{2,1,0:T(8,128)(2,1)}, s32[]{:T(128)}, bf16[128,320]{1,0:T(8,128)(2,1)S(1)}, ...), branch_computations={%region_14.14_spmd, %region_15.20_spmd} | conditional | flops 106823296 | bytes 5106229 | solution.py:219
  156.4 5.1 %conditional.12 = (f32[128,320]{1,0:T(8,128)S(1)}, f32[640,320]{0,1:T(8,128)S(1)}, f32[640]{0:T(1024)S(1)}, bf16[128,320]{1,0:T(8,128)(2,1)S(1)}) conditional(s32[]{:T(128)} %convert_element_type.275, () %tuple.212, (pred[]{:T(512)}, bf16[4,128,320]{2,1,0:T(8,128)(2,1)}, s32[]{:T(128)}, bf16[128,320]{1,0:T(8,128)(2,1)S(1)}, ...), branch_computations={%region_14.14_spmd, %region_15.20_spmd} | conditional | flops 106823296 | bytes 5106229 | solution.py:219
  166.8 5.1 %conditional.12 = (f32[128,320]{1,0:T(8,128)S(1)}, f32[640,320]{0,1:T(8,128)S(1)}, f32[640]{0:T(1024)S(1)}, bf16[128,320]{1,0:T(8,128)(2,1)S(1)}) conditional(s32[]{:T(128)} %convert_element_type.275, () %tuple.212, (pred[]{:T(512)}, bf16[4,128,320]{2,1,0:T(8,128)(2,1)}, s32[]{:T(128)}, bf16[128,320]{1,0:T(8,128)(2,1)S(1)}, ...), branch_computations={%region_14.14_spmd, %region_15.20_spmd} | conditional | flops 106823296 | bytes 5106229 | solution.py:219
  171.9 1.3 collective-permute-start.2
  177.3 5.1 %conditional.12 = (f32[128,320]{1,0:T(8,128)S(1)}, f32[640,320]{0,1:T(8,128)S(1)}, f32[640]{0:T(1024)S(1)}, bf16[128,320]{1,0:T(8,128)(2,1)S(1)}) conditional(s32[]{:T(128)} %convert_element_type.275, () %tuple.212, (pred[]{:T(512)}, bf16[4,128,320]{2,1,0:T(8,128)(2,1)}, s32[]{:T(128)}, bf16[128,320]{1,0:T(8,128)(2,1)S(1)}, ...), branch_computations={%region_14.14_spmd, %region_15.20_spmd} | conditional | flops 106823296 | bytes 5106229 | solution.py:219
  188.6 73.6 %while.83 = (s32[]{:T(128)}, bf16[128,320]{0,1:T(8,128)(2,1)S(1)}, f32[320,1280]{1,0:T(8,128)}, f32[1280,320]{0,1:T(8,128)}, f32[320]{0:T(512)S(1)}, /*index=5*/...) while((s32[]{:T(128)}, bf16[128,320]{0,1:T(8,128)(2,1)S(1)}, ...), condition=%wide.region_28.29_spmd.clone, body=%wide.region_22.28_spmd.clone.sunk | while | flops 531784128 | bytes 38364704 | solution.py:278
  188.6 7.3 %conditional.13 = (f32[128,320]{0,1:T(8,128)S(1)}, f32[320,1280]{1,0:T(8,128)S(1)}, f32[1280,320]{0,1:T(8,128)S(1)}, f32[320]{0:T(512)S(1)}) conditional(s32[]{:T(128)} %convert_element_type.277, () %tuple.215, (pred[]{:T(512)}, bf16[4,128,320]{1,2,0:T(8,128)(2,1)}, s32[]{:T(128)}, bf16[128,320]{0,1:T(8,128)(2,1)S(1)}, ...), branch_computations={%region_23.23_spmd, %region_24.27_spmd} | conditional | flops 530063168 | bytes 14685557 | solution.py:239
  190.6 1.7 fusion.81
  193.3 1.6 fusion.73
  196.0 1.6 fusion.110
  198.8 1.4 select_add_fusion.12
  202.5 7.4 %conditional.13 = (f32[128,320]{0,1:T(8,128)S(1)}, f32[320,1280]{1,0:T(8,128)S(1)}, f32[1280,320]{0,1:T(8,128)S(1)}, f32[320]{0:T(512)S(1)}) conditional(s32[]{:T(128)} %convert_element_type.277, () %tuple.215, (pred[]{:T(512)}, bf16[4,128,320]{1,2,0:T(8,128)(2,1)}, s32[]{:T(128)}, bf16[128,320]{0,1:T(8,128)(2,1)S(1)}, ...), branch_computations={%region_23.23_spmd, %region_24.27_spmd} | conditional | flops 530063168 | bytes 14685557 | solution.py:239
  204.5 1.7 fusion.81
  207.2 1.6 fusion.73
  209.9 1.6 fusion.110
  211.5 1.7 collective-permute-start.3
  213.2 2.9 select_add_fusion.12
  217.7 7.4 %conditional.13 = (f32[128,320]{0,1:T(8,128)S(1)}, f32[320,1280]{1,0:T(8,128)S(1)}, f32[1280,320]{0,1:T(8,128)S(1)}, f32[320]{0:T(512)S(1)}) conditional(s32[]{:T(128)} %convert_element_type.277, () %tuple.215, (pred[]{:T(512)}, bf16[4,128,320]{1,2,0:T(8,128)(2,1)}, s32[]{:T(128)}, bf16[128,320]{0,1:T(8,128)(2,1)S(1)}, ...), branch_computations={%region_23.23_spmd, %region_24.27_spmd} | conditional | flops 530063168 | bytes 14685557 | solution.py:239
  219.8 1.7 fusion.81
  222.5 1.6 fusion.73
  225.1 1.6 fusion.110
  228.0 2.9 select_add_fusion.12
  232.6 7.4 %conditional.13 = (f32[128,320]{0,1:T(8,128)S(1)}, f32[320,1280]{1,0:T(8,128)S(1)}, f32[1280,320]{0,1:T(8,128)S(1)}, f32[320]{0:T(512)S(1)}) conditional(s32[]{:T(128)} %convert_element_type.277, () %tuple.215, (pred[]{:T(512)}, bf16[4,128,320]{1,2,0:T(8,128)(2,1)}, s32[]{:T(128)}, bf16[128,320]{0,1:T(8,128)(2,1)S(1)}, ...), branch_computations={%region_23.23_spmd, %region_24.27_spmd} | conditional | flops 530063168 | bytes 14685557 | solution.py:239
  234.6 1.7 fusion.81
  237.3 1.6 fusion.73
  240.0 1.6 fusion.110
  242.8 2.9 select_add_fusion.12
  247.7 1.6 fusion.110
  249.3 8.4 %collective-permute-start.3 = (bf16[128,320]{0,1:T(8,128)(2,1)}, bf16[128,320]{0,1:T(8,128)(2,1)S(1)}, u32[]{:S(2)}, u32[]{:S(2)}) collective-permute-start(bf16[128,320]{0,1:T(8,128)(2,1)} %fusion.110), channel_id=1, source_target_pairs={{1,0},{3,2},{5,4},{7,6},{9,8},{11,10},{13,12},{15,14},{17,16},{19,... | collective-permute-start | bytes 245768 | tf_op jit(solution)/shard_map/while/body/eval_jaxpr/ppermute | solution.py:16
  257.7 2.9 select_add_fusion.12
  262.2 104.7 %all-reduce.2 = (bf16[320,1280]{1,0:T(8,128)(2,1)}, bf16[1280,320]{0,1:T(8,128)(2,1)}, f32[1,320]{1,0:T(1,128)}, bf16[640,320]{0,1:T(8,128)(2,1)}, f32[1,640]{1,0:T(1,128)}) all-reduce(f32[320,1280]{1,0:T(8,128)} %get-tuple-element.1305, f32[1280,320]{0,1:T(8,128)} %get-tuple-element.1306, ...), channel_id=1, replica_groups=mesh['dp'=16,'pipe'=2] {'dp'}, use_global_device_ids=true, to_apply=%region_29.30 | all-reduce | flops 1024960 | bytes 6151680 | tf_op jit(solution)/shard_map/psum | solution.py:286
  (368 shorter events, 98.2 us)
Async XLA Ops:
  3.6 3.4 copy-start.10
  6.1 0.7 copy-start.5
  7.0 2.6 copy-start.11
  9.8 6.2 %collective-permute-start = (bf16[128,320]{0,1:T(8,128)(2,1)S(1)}, bf16[128,320]{0,1:T(8,128)(2,1)S(1)}, u32[]{:S(2)}, u32[]{:S(2)}) collective-permute-start(bf16[128,320]{0,1:T(8,128)(2,1)S(1)} %get-tuple-element.2172), channel_id=1, source_target_pairs={{0,1},{2,3},{4,5},{6,7},{8,9},{10,11},{12,13},{14,15},{16,17},{18,... | collective-permute-start | bytes 245768 | tf_op jit(solution)/shard_map/while/body/eval_jaxpr/ppermute | solution.py:16
  18.6 5.2 %collective-permute-start = (bf16[128,320]{0,1:T(8,128)(2,1)S(1)}, bf16[128,320]{0,1:T(8,128)(2,1)S(1)}, u32[]{:S(2)}, u32[]{:S(2)}) collective-permute-start(bf16[128,320]{0,1:T(8,128)(2,1)S(1)} %get-tuple-element.2172), channel_id=1, source_target_pairs={{0,1},{2,3},{4,5},{6,7},{8,9},{10,11},{12,13},{14,15},{16,17},{18,... | collective-permute-start | bytes 245768 | tf_op jit(solution)/shard_map/while/body/eval_jaxpr/ppermute | solution.py:16
  26.4 5.2 %collective-permute-start = (bf16[128,320]{0,1:T(8,128)(2,1)S(1)}, bf16[128,320]{0,1:T(8,128)(2,1)S(1)}, u32[]{:S(2)}, u32[]{:S(2)}) collective-permute-start(bf16[128,320]{0,1:T(8,128)(2,1)S(1)} %get-tuple-element.2172), channel_id=1, source_target_pairs={{0,1},{2,3},{4,5},{6,7},{8,9},{10,11},{12,13},{14,15},{16,17},{18,... | collective-permute-start | bytes 245768 | tf_op jit(solution)/shard_map/while/body/eval_jaxpr/ppermute | solution.py:16
  34.2 5.2 %collective-permute-start = (bf16[128,320]{0,1:T(8,128)(2,1)S(1)}, bf16[128,320]{0,1:T(8,128)(2,1)S(1)}, u32[]{:S(2)}, u32[]{:S(2)}) collective-permute-start(bf16[128,320]{0,1:T(8,128)(2,1)S(1)} %get-tuple-element.2172), channel_id=1, source_target_pairs={{0,1},{2,3},{4,5},{6,7},{8,9},{10,11},{12,13},{14,15},{16,17},{18,... | collective-permute-start | bytes 245768 | tf_op jit(solution)/shard_map/while/body/eval_jaxpr/ppermute | solution.py:16
  42.0 5.2 %collective-permute-start = (bf16[128,320]{0,1:T(8,128)(2,1)S(1)}, bf16[128,320]{0,1:T(8,128)(2,1)S(1)}, u32[]{:S(2)}, u32[]{:S(2)}) collective-permute-start(bf16[128,320]{0,1:T(8,128)(2,1)S(1)} %get-tuple-element.2172), channel_id=1, source_target_pairs={{0,1},{2,3},{4,5},{6,7},{8,9},{10,11},{12,13},{14,15},{16,17},{18,... | collective-permute-start | bytes 245768 | tf_op jit(solution)/shard_map/while/body/eval_jaxpr/ppermute | solution.py:16
  48.2 2.8 collective-permute-start.1
  51.8 5.9 %collective-permute-start.1 = (bf16[128,320]{0,1:T(8,128)(2,1)S(1)}, bf16[128,320]{0,1:T(8,128)(2,1)S(1)}, u32[]{:S(2)}, u32[]{:S(2)}) collective-permute-start(bf16[128,320]{0,1:T(8,128)(2,1)S(1)} %get-tuple-element.2173), channel_id=1, source_target_pairs={{1,0},{3,2},{5,4},{7,6},{9,8},{11,10},{13,12},{15,14},{17,16},{19,... | collective-permute-start | bytes 245768 | tf_op jit(solution)/shard_map/while/body/eval_jaxpr/ppermute | solution.py:16
  58.6 5.6 %collective-permute-start.1 = (bf16[128,320]{0,1:T(8,128)(2,1)S(1)}, bf16[128,320]{0,1:T(8,128)(2,1)S(1)}, u32[]{:S(2)}, u32[]{:S(2)}) collective-permute-start(bf16[128,320]{0,1:T(8,128)(2,1)S(1)} %get-tuple-element.2173), channel_id=1, source_target_pairs={{1,0},{3,2},{5,4},{7,6},{9,8},{11,10},{13,12},{15,14},{17,16},{19,... | collective-permute-start | bytes 245768 | tf_op jit(solution)/shard_map/while/body/eval_jaxpr/ppermute | solution.py:16
  65.0 5.5 %collective-permute-start.1 = (bf16[128,320]{0,1:T(8,128)(2,1)S(1)}, bf16[128,320]{0,1:T(8,128)(2,1)S(1)}, u32[]{:S(2)}, u32[]{:S(2)}) collective-permute-start(bf16[128,320]{0,1:T(8,128)(2,1)S(1)} %get-tuple-element.2173), channel_id=1, source_target_pairs={{1,0},{3,2},{5,4},{7,6},{9,8},{11,10},{13,12},{15,14},{17,16},{19,... | collective-permute-start | bytes 245768 | tf_op jit(solution)/shard_map/while/body/eval_jaxpr/ppermute | solution.py:16
  70.6 5.9 %collective-permute-start.1 = (bf16[128,320]{0,1:T(8,128)(2,1)S(1)}, bf16[128,320]{0,1:T(8,128)(2,1)S(1)}, u32[]{:S(2)}, u32[]{:S(2)}) collective-permute-start(bf16[128,320]{0,1:T(8,128)(2,1)S(1)} %get-tuple-element.2173), channel_id=1, source_target_pairs={{1,0},{3,2},{5,4},{7,6},{9,8},{11,10},{13,12},{15,14},{17,16},{19,... | collective-permute-start | bytes 245768 | tf_op jit(solution)/shard_map/while/body/eval_jaxpr/ppermute | solution.py:16
  76.5 0.7 copy-start.7
  76.5 0.8 copy-start.8
  76.5 59.9 %copy-start.2 = (bf16[4,128,320]{1,2,0:T(8,128)(2,1)}, bf16[4,128,320]{1,2,0:T(8,128)(2,1)S(1)}, u32[]{:S(2)}) copy-start(bf16[4,128,320]{1,2,0:T(8,128)(2,1)S(1)} %get-tuple-element.2175) | copy-start | bytes 983044
  76.5 3.9 %copy-start.6 = (bf16[4,128,320]{2,1,0:T(8,128)(2,1)S(1)}, bf16[4,128,320]{2,1,0:T(8,128)(2,1)}, u32[]{:S(2)}) copy-start(bf16[4,128,320]{2,1,0:T(8,128)(2,1)} %copy-done.5) | copy-start | bytes 983044
  80.4 57.7 %copy-start.12 = (f32[1,640]{1,0:T(1,128)S(1)}, f32[1,640]{1,0:T(1,128)}, u32[]{:S(2)}) copy-start(f32[1,640]{1,0:T(1,128)} %param.33) | copy-start | bytes 7684
  138.2 7.7 %collective-permute-start.2 = (bf16[128,320]{1,0:T(8,128)(2,1)S(1)}, bf16[128,320]{1,0:T(8,128)(2,1)S(1)}, u32[]{:S(2)}, u32[]{:S(2)}) collective-permute-start(bf16[128,320]{1,0:T(8,128)(2,1)S(1)} %get-tuple-element.1924), channel_id=1, source_target_pairs={{0,1},{2,3},{4,5},{6,7},{8,9},{10,11},{12,13},{14,15},{16,17},{18,... | collective-permute-start | bytes 245768 | tf_op jit(solution)/shard_map/while/body/eval_jaxpr/ppermute | solution.py:16
  151.0 5.4 %collective-permute-start.2 = (bf16[128,320]{1,0:T(8,128)(2,1)S(1)}, bf16[128,320]{1,0:T(8,128)(2,1)S(1)}, u32[]{:S(2)}, u32[]{:S(2)}) collective-permute-start(bf16[128,320]{1,0:T(8,128)(2,1)S(1)} %get-tuple-element.1924), channel_id=1, source_target_pairs={{0,1},{2,3},{4,5},{6,7},{8,9},{10,11},{12,13},{14,15},{16,17},{18,... | collective-permute-start | bytes 245768 | tf_op jit(solution)/shard_map/while/body/eval_jaxpr/ppermute | solution.py:16
  161.5 5.4 %collective-permute-start.2 = (bf16[128,320]{1,0:T(8,128)(2,1)S(1)}, bf16[128,320]{1,0:T(8,128)(2,1)S(1)}, u32[]{:S(2)}, u32[]{:S(2)}) collective-permute-start(bf16[128,320]{1,0:T(8,128)(2,1)S(1)} %get-tuple-element.1924), channel_id=1, source_target_pairs={{0,1},{2,3},{4,5},{6,7},{8,9},{10,11},{12,13},{14,15},{16,17},{18,... | collective-permute-start | bytes 245768 | tf_op jit(solution)/shard_map/while/body/eval_jaxpr/ppermute | solution.py:16
  171.9 5.4 %collective-permute-start.2 = (bf16[128,320]{1,0:T(8,128)(2,1)S(1)}, bf16[128,320]{1,0:T(8,128)(2,1)S(1)}, u32[]{:S(2)}, u32[]{:S(2)}) collective-permute-start(bf16[128,320]{1,0:T(8,128)(2,1)S(1)} %get-tuple-element.1924), channel_id=1, source_target_pairs={{0,1},{2,3},{4,5},{6,7},{8,9},{10,11},{12,13},{14,15},{16,17},{18,... | collective-permute-start | bytes 245768 | tf_op jit(solution)/shard_map/while/body/eval_jaxpr/ppermute | solution.py:16
  182.4 5.4 %collective-permute-start.2 = (bf16[128,320]{1,0:T(8,128)(2,1)S(1)}, bf16[128,320]{1,0:T(8,128)(2,1)S(1)}, u32[]{:S(2)}, u32[]{:S(2)}) collective-permute-start(bf16[128,320]{1,0:T(8,128)(2,1)S(1)} %get-tuple-element.1924), channel_id=1, source_target_pairs={{0,1},{2,3},{4,5},{6,7},{8,9},{10,11},{12,13},{14,15},{16,17},{18,... | collective-permute-start | bytes 245768 | tf_op jit(solution)/shard_map/while/body/eval_jaxpr/ppermute | solution.py:16
  187.7 0.9 copy-start.4
  188.6 3.7 %copy-start.9 = (bf16[1280,320]{1,0:T(8,128)(2,1)S(1)}, bf16[1280,320]{1,0:T(8,128)(2,1)}, u32[]{:S(2)}) copy-start(bf16[1280,320]{1,0:T(8,128)(2,1)} %get-tuple-element.1258) | copy-start | bytes 2457604 | tf_op jit(solution)/shard_map/while/body/eval_jaxpr/cond
  192.3 1.0 copy-start.3
  197.5 4.9 %collective-permute-start.3 = (bf16[128,320]{0,1:T(8,128)(2,1)}, bf16[128,320]{0,1:T(8,128)(2,1)S(1)}, u32[]{:S(2)}, u32[]{:S(2)}) collective-permute-start(bf16[128,320]{0,1:T(8,128)(2,1)} %fusion.110), channel_id=1, source_target_pairs={{1,0},{3,2},{5,4},{7,6},{9,8},{11,10},{13,12},{15,14},{17,16},{19,... | collective-permute-start | bytes 245768 | tf_op jit(solution)/shard_map/while/body/eval_jaxpr/ppermute | solution.py:16
  198.8 2.0 copy-start
  201.3 1.2 copy-start.1
  202.5 3.7 %copy-start.9 = (bf16[1280,320]{1,0:T(8,128)(2,1)S(1)}, bf16[1280,320]{1,0:T(8,128)(2,1)}, u32[]{:S(2)}) copy-start(bf16[1280,320]{1,0:T(8,128)(2,1)} %get-tuple-element.1258) | copy-start | bytes 2457604 | tf_op jit(solution)/shard_map/while/body/eval_jaxpr/cond
  206.2 1.0 copy-start.3
  211.5 6.3 %collective-permute-start.3 = (bf16[128,320]{0,1:T(8,128)(2,1)}, bf16[128,320]{0,1:T(8,128)(2,1)S(1)}, u32[]{:S(2)}, u32[]{:S(2)}) collective-permute-start(bf16[128,320]{0,1:T(8,128)(2,1)} %fusion.110), channel_id=1, source_target_pairs={{1,0},{3,2},{5,4},{7,6},{9,8},{11,10},{13,12},{15,14},{17,16},{19,... | collective-permute-start | bytes 245768 | tf_op jit(solution)/shard_map/while/body/eval_jaxpr/ppermute | solution.py:16
  213.1 3.0 copy-start
  216.5 1.2 copy-start.1
  217.8 3.7 %copy-start.9 = (bf16[1280,320]{1,0:T(8,128)(2,1)S(1)}, bf16[1280,320]{1,0:T(8,128)(2,1)}, u32[]{:S(2)}) copy-start(bf16[1280,320]{1,0:T(8,128)(2,1)} %get-tuple-element.1258) | copy-start | bytes 2457604 | tf_op jit(solution)/shard_map/while/body/eval_jaxpr/cond
  221.5 1.0 copy-start.3
  226.7 5.9 %collective-permute-start.3 = (bf16[128,320]{0,1:T(8,128)(2,1)}, bf16[128,320]{0,1:T(8,128)(2,1)S(1)}, u32[]{:S(2)}, u32[]{:S(2)}) collective-permute-start(bf16[128,320]{0,1:T(8,128)(2,1)} %fusion.110), channel_id=1, source_target_pairs={{1,0},{3,2},{5,4},{7,6},{9,8},{11,10},{13,12},{15,14},{17,16},{19,... | collective-permute-start | bytes 245768 | tf_op jit(solution)/shard_map/while/body/eval_jaxpr/ppermute | solution.py:16
  228.0 3.0 copy-start
  231.4 1.2 copy-start.1
  232.6 3.7 %copy-start.9 = (bf16[1280,320]{1,0:T(8,128)(2,1)S(1)}, bf16[1280,320]{1,0:T(8,128)(2,1)}, u32[]{:S(2)}) copy-start(bf16[1280,320]{1,0:T(8,128)(2,1)} %get-tuple-element.1258) | copy-start | bytes 2457604 | tf_op jit(solution)/shard_map/while/body/eval_jaxpr/cond
  236.3 1.0 copy-start.3
  241.5 5.9 %collective-permute-start.3 = (bf16[128,320]{0,1:T(8,128)(2,1)}, bf16[128,320]{0,1:T(8,128)(2,1)S(1)}, u32[]{:S(2)}, u32[]{:S(2)}) collective-permute-start(bf16[128,320]{0,1:T(8,128)(2,1)} %fusion.110), channel_id=1, source_target_pairs={{1,0},{3,2},{5,4},{7,6},{9,8},{11,10},{13,12},{15,14},{17,16},{19,... | collective-permute-start | bytes 245768 | tf_op jit(solution)/shard_map/while/body/eval_jaxpr/ppermute | solution.py:16
  242.8 3.0 copy-start
  246.2 1.2 copy-start.1
  249.3 12.9 %collective-permute-start.3 = (bf16[128,320]{0,1:T(8,128)(2,1)}, bf16[128,320]{0,1:T(8,128)(2,1)S(1)}, u32[]{:S(2)}, u32[]{:S(2)}) collective-permute-start(bf16[128,320]{0,1:T(8,128)(2,1)} %fusion.110), channel_id=1, source_target_pairs={{1,0},{3,2},{5,4},{7,6},{9,8},{11,10},{13,12},{15,14},{17,16},{19,... | collective-permute-start | bytes 245768 | tf_op jit(solution)/shard_map/while/body/eval_jaxpr/ppermute | solution.py:16
  257.7 3.0 copy-start
  261.0 1.2 copy-start.1
where the time goes:
time: 371 us; the launch traced here: 368 us
  blocking collectives  156 us (42%)
  other arithmetic  58.6 us (16%)
  starting transfers between devices  44.4 us (12%)
  local copies, waits for them, and re-layouts  40.8 us (11%)
  matrix products  32.7 us (9%)
  waiting for transfers between devices  30.7 us (8%)
    psum x1, blocking collectives, body(): lax.psum((enc_sums[0], enc_sums[1], enc_sums[2], dec_sums[0], dec_sums[1]...  105 us
    psum x1, blocking collectives, body(): loss_value = lax.psum(local_sum, ('dp', 'pipe')) / (total_rows * channels)  51.1 us
    ppermute x20, starting transfers between devices, from_behind(): return lax.ppermute(shard, axis, pairs)  44.4 us
    ppermute x20, waiting for transfers between devices, from_behind(): return lax.ppermute(shard, axis, pairs)  30.7 us
    add x5, other arithmetic, backward_tick(): enc_sums[0] + grad_in  13.1 us
    dynamic_slice x48, local copies, waits for them, and re-layouts, take_slot(): return lax.dynamic_index_in_dim(buffer, slot_index, 0, keepdims=False)  10.9 us
    dot_general x12, matrix products, right_dot(): lax.dot_general(matrix_a, matrix_b, (((1,), (1,)), ((), ())), preferred_e...  9.99 us
    dot_general x4, matrix products, encode(): jnp.dot(hidden, weight_out, preferred_element_type=jnp.float32)  9.62 us
  transfers between devices with their start and end apart: 20, of which 15 were waited for; matrix products, arithmetic and copies ran while one was open for 10% of the time, Pallas kernels for 0%

commit v1 on v0

--- a/solution.py
+++ b/solution.py
@@ -206,7 +206,9 @@
     pred_rows = loop_state[5]
     residual = pred_rows.astype(jnp.float32) - target
     local_sum = jnp.where(is_first, jnp.sum(residual * residual), jnp.float32(0.0))
-    loss_value = lax.psum(local_sum, ("dp", "pipe")) / (total_rows * channels)
+    loss_value = jnp.sum(lax.all_gather(local_sum, ("dp", "pipe")), axis=0) / (
+        total_rows * channels
+    )
     grad_seed = (residual / math.sqrt(total_rows)).astype(jnp.bfloat16)
 
     def backward_tick(tick, loop_state, offset, run_up, run_down):

time: 371 us -> 358 us (0.965)
  local copies, waits for them, and re-layouts: 40.8 us -> 27.4 us
  other arithmetic: 58.6 us -> 62.4 us
    psum x1 -> x0, blocking collectives: 51.1 us -> none  [body(): loss_value = lax.psum(local_sum, ('dp', 'pipe')) / (total_rows * channels)]
    unnamed x0 -> x1, blocking collectives: none -> 50.8 us
    add x5, other arithmetic: 2.12 us -> 12.7 us  [backward_tick(): enc_sums[1] + grad_out]
    add x10, other arithmetic: 1.07 us -> 9.5 us  [backward_tick(): dec_sums = (dec_sums[0] + grad_weight, dec_sums[1] + grad_gain)]
    select_n x4, other arithmetic: 3.94 us -> 0.04 us  [backward_tick(): grad_y = jnp.where(is_last, take_slot(top_grads, slot_index), recv_down)]
    unnamed x24 -> x26, local copies, waits for them, and re-layouts: 9.24 us -> 5.95 us
  transfers between devices with their start and end apart: 20 -> 20, of which waited for: 15 -> 11; matrix products, arithmetic and copies ran while one was open for 10% -> 13% of each run, Pallas kernels for 0% -> 0%
where the time goes in v1:
time: 358 us; the launch traced here: 355 us
  blocking collectives  153 us (43%)
  other arithmetic  62.4 us (17%)
  starting transfers between devices  45.1 us (13%)
  matrix products  32.7 us (9%)
  waiting for transfers between devices  28.6 us (8%)
  local copies, waits for them, and re-layouts  27.4 us (8%)
    psum x1, blocking collectives, body(): lax.psum((enc_sums[0], enc_sums[1], enc_sums[2], dec_sums[0], dec_sums[1]...  102 us
    unnamed x1, blocking collectives  50.8 us
    ppermute x20, starting transfers between devices, from_behind(): return lax.ppermute(shard, axis, pairs)  45.1 us
    ppermute x20, waiting for transfers between devices, from_behind(): return lax.ppermute(shard, axis, pairs)  28.6 us
    add x5, other arithmetic, backward_tick(): enc_sums[1] + grad_out  12.7 us
    add x5, other arithmetic, backward_tick(): enc_sums[0] + grad_in  12.7 us
    dot_general x12, matrix products, right_dot(): lax.dot_general(matrix_a, matrix_b, (((1,), (1,)), ((), ())), preferred_e...  9.98 us
    dot_general x4, matrix products, encode(): jnp.dot(hidden, weight_out, preferred_element_type=jnp.float32)  9.62 us
  transfers between devices with their start and end apart: 20, of which 11 were waited for; matrix products, arithmetic and copies ran while one was open for 13% of the time, Pallas kernels for 0%

profile of v1, /device:TPU:19, one launch (start us, length us, event | category | flops | bytes accessed | tf_op | source)
XLA Modules:
  0.0 354.5 jit_solution(12865316952814536737)
XLA Ops:
  6.9 2.2 copy.17
  9.2 37.5 %while.80 = (s32[]{:T(128)}, bf16[128,320]{0,1:T(8,128)(2,1)S(1)}, bf16[4,128,320]{1,2,0:T(8,128)(2,1)S(1)}, bf16[4,128,320]{1,2,0:T(8,128)(2,1)S(1)}, s32[]{:T(...) while((s32[]{:T(128)}, bf16[128,320]{0,1:T(8,128)(2,1)S(1)}, ...), condition=%wide.region_4.5_spmd, body=%wide.region_0.4_spmd.sunk | while | flops 211763328 | bytes 3204945 | solution.py:192
  10.7 4.8 %collective-permute-done = bf16[128,320]{0,1:T(8,128)(2,1)S(1)} collective-permute-done((bf16[128,320]{0,1:T(8,128)(2,1)S(1)}, bf16[128,320]{0,1:T(8,128)(2,1)S(1)}, u32[]{:S(2)}, u32[]{:S(2)}) %collective-permute-start) | collective-permute-done | bytes 81952 | tf_op jit(solution)/shard_map/while/body/eval_jaxpr/ppermute | solution.py:16
  15.6 2.5 conditional.10
  15.7 2.4 fusion.11
  19.5 3.8 %collective-permute-done = bf16[128,320]{0,1:T(8,128)(2,1)S(1)} collective-permute-done((bf16[128,320]{0,1:T(8,128)(2,1)S(1)}, bf16[128,320]{0,1:T(8,128)(2,1)S(1)}, u32[]{:S(2)}, u32[]{:S(2)}) %collective-permute-start) | collective-permute-done | bytes 81952 | tf_op jit(solution)/shard_map/while/body/eval_jaxpr/ppermute | solution.py:16
  23.4 2.5 conditional.10
  23.5 2.4 fusion.11
  27.3 3.8 %collective-permute-done = bf16[128,320]{0,1:T(8,128)(2,1)S(1)} collective-permute-done((bf16[128,320]{0,1:T(8,128)(2,1)S(1)}, bf16[128,320]{0,1:T(8,128)(2,1)S(1)}, u32[]{:S(2)}, u32[]{:S(2)}) %collective-permute-start) | collective-permute-done | bytes 81952 | tf_op jit(solution)/shard_map/while/body/eval_jaxpr/ppermute | solution.py:16
  31.2 2.5 conditional.10
  31.3 2.4 fusion.11
  35.1 3.8 %collective-permute-done = bf16[128,320]{0,1:T(8,128)(2,1)S(1)} collective-permute-done((bf16[128,320]{0,1:T(8,128)(2,1)S(1)}, bf16[128,320]{0,1:T(8,128)(2,1)S(1)}, u32[]{:S(2)}, u32[]{:S(2)}) %collective-permute-start) | collective-permute-done | bytes 81952 | tf_op jit(solution)/shard_map/while/body/eval_jaxpr/ppermute | solution.py:16
  39.0 2.5 conditional.10
  39.1 2.4 fusion.11
  42.9 3.8 %collective-permute-done = bf16[128,320]{0,1:T(8,128)(2,1)S(1)} collective-permute-done((bf16[128,320]{0,1:T(8,128)(2,1)S(1)}, bf16[128,320]{0,1:T(8,128)(2,1)S(1)}, u32[]{:S(2)}, u32[]{:S(2)}) %collective-permute-start) | collective-permute-done | bytes 81952 | tf_op jit(solution)/shard_map/while/body/eval_jaxpr/ppermute | solution.py:16
  47.3 29.1 %while.81 = (s32[]{:T(128)}, bf16[128,320]{0,1:T(8,128)(2,1)S(1)}, bf16[4,128,320]{1,2,0:T(8,128)(2,1)S(1)}, bf16[4,128,320]{1,2,0:T(8,128)(2,1)S(1)}, s32[]{:T(...) while((s32[]{:T(128)}, bf16[128,320]{0,1:T(8,128)(2,1)S(1)}, ...), condition=%wide.region_10.11_spmd, body=%wide.region_5.10_spmd.sunk | while | flops 53575944 | bytes 2551637 | solution.py:198
  49.5 1.4 collective-permute-done.1
  51.8 3.7 %collective-permute-start.1 = (bf16[128,320]{0,1:T(8,128)(2,1)S(1)}, bf16[128,320]{0,1:T(8,128)(2,1)S(1)}, u32[]{:S(2)}, u32[]{:S(2)}) collective-permute-start(bf16[128,320]{0,1:T(8,128)(2,1)S(1)} %get-tuple-element.2173), channel_id=1, source_target_pairs={{1,0},{3,2},{5,4},{7,6},{9,8},{11,10},{13,12},{15,14},{17,16},{19,... | collective-permute-start | bytes 245768 | tf_op jit(solution)/shard_map/while/body/eval_jaxpr/ppermute | solution.py:16
  55.5 2.2 collective-permute-done.1
  58.5 4.1 %collective-permute-start.1 = (bf16[128,320]{0,1:T(8,128)(2,1)S(1)}, bf16[128,320]{0,1:T(8,128)(2,1)S(1)}, u32[]{:S(2)}, u32[]{:S(2)}) collective-permute-start(bf16[128,320]{0,1:T(8,128)(2,1)S(1)} %get-tuple-element.2173), channel_id=1, source_target_pairs={{1,0},{3,2},{5,4},{7,6},{9,8},{11,10},{13,12},{15,14},{17,16},{19,... | collective-permute-start | bytes 245768 | tf_op jit(solution)/shard_map/while/body/eval_jaxpr/ppermute | solution.py:16
  62.7 1.4 collective-permute-done.1
  64.9 4.0 %collective-permute-start.1 = (bf16[128,320]{0,1:T(8,128)(2,1)S(1)}, bf16[128,320]{0,1:T(8,128)(2,1)S(1)}, u32[]{:S(2)}, u32[]{:S(2)}) collective-permute-start(bf16[128,320]{0,1:T(8,128)(2,1)S(1)} %get-tuple-element.2173), channel_id=1, source_target_pairs={{1,0},{3,2},{5,4},{7,6},{9,8},{11,10},{13,12},{15,14},{17,16},{19,... | collective-permute-start | bytes 245768 | tf_op jit(solution)/shard_map/while/body/eval_jaxpr/ppermute | solution.py:16
  70.5 4.4 %collective-permute-start.1 = (bf16[128,320]{0,1:T(8,128)(2,1)S(1)}, bf16[128,320]{0,1:T(8,128)(2,1)S(1)}, u32[]{:S(2)}, u32[]{:S(2)}) collective-permute-start(bf16[128,320]{0,1:T(8,128)(2,1)S(1)} %get-tuple-element.2173), channel_id=1, source_target_pairs={{1,0},{3,2},{5,4},{7,6},{9,8},{11,10},{13,12},{15,14},{17,16},{19,... | collective-permute-start | bytes 245768 | tf_op jit(solution)/shard_map/while/body/eval_jaxpr/ppermute | solution.py:16
  76.9 1.7 multiply_convert_fusion.4
  79.4 50.8 %all-reduce = f32[32]{0:T(128)S(1)} all-reduce(f32[32]{0:T(128)S(1)} %dynamic-update-slice), channel_id=1, replica_groups=mesh['dp'=16,'pipe'=2] {'dp','pipe'}, use_global_device_ids=true, to_apply=%add | all-reduce | flops 32 | bytes 256
  132.7 37.9 %while.82 = (s32[]{:T(128)}, bf16[128,320]{1,0:T(8,128)(2,1)S(1)}, f32[4,128,320]{1,2,0:T(8,128)}, bf16[4,128,320]{1,2,0:T(8,128)(2,1)S(1)}, f32[640,320]{0,1:T(...) while((s32[]{:T(128)}, bf16[128,320]{1,0:T(8,128)(2,1)S(1)}, ...), condition=%wide.region_21.22_spmd.clone, body=%wide.region_13.21_spmd.clone.sunk | while | flops 107316104 | bytes 10603436 | solution.py:274
  138.2 2.4 conditional.12
  144.1 2.1 select_add_fusion.10
  146.2 2.4 conditional.12
  152.2 2.1 select_add_fusion.10
  154.4 2.4 conditional.12
  160.3 2.1 select_add_fusion.10
  162.5 2.4 conditional.12
  168.4 2.1 select_add_fusion.10
  170.6 80.6 %while.83 = (s32[]{:T(128)}, bf16[128,320]{0,1:T(8,128)(2,1)S(1)}, f32[320,1280]{1,0:T(8,128)}, f32[1280,320]{0,1:T(8,128)}, f32[320]{0:T(512)S(1)}, /*index=5*/...) while((s32[]{:T(128)}, bf16[128,320]{0,1:T(8,128)(2,1)S(1)}, ...), condition=%wide.region_28.29_spmd.clone, body=%wide.region_22.28_spmd.clone.sunk | while | flops 531784128 | bytes 27878944 | solution.py:280
  171.4 7.1 %conditional.13 = (f32[128,320]{0,1:T(8,128)S(1)}, f32[320,1280]{1,0:T(8,128)S(1)}, f32[1280,320]{0,1:T(8,128)S(1)}, f32[320]{0:T(512)S(1)}) conditional(s32[]{:T(128)} %convert_element_type.277, () %tuple.215, (pred[]{:T(512)}, bf16[4,128,320]{1,2,0:T(8,128)(2,1)S(1)}, s32[]{:T(128)}, bf16[128,320]{0,1:T(8,128)(2,1)S(1)}, ...), branch_computations={%region_23.23_spmd, %region_24.27_spmd} | conditional | flops 530063168 | bytes 14685557 | solution.py:241
  173.2 1.7 fusion.81
  175.9 1.6 fusion.73
  178.5 1.6 fusion.110
  181.4 1.4 select_add_fusion.12
  184.9 7.1 %conditional.13 = (f32[128,320]{0,1:T(8,128)S(1)}, f32[320,1280]{1,0:T(8,128)S(1)}, f32[1280,320]{0,1:T(8,128)S(1)}, f32[320]{0:T(512)S(1)}) conditional(s32[]{:T(128)} %convert_element_type.277, () %tuple.215, (pred[]{:T(512)}, bf16[4,128,320]{1,2,0:T(8,128)(2,1)S(1)}, s32[]{:T(128)}, bf16[128,320]{0,1:T(8,128)(2,1)S(1)}, ...), branch_computations={%region_23.23_spmd, %region_24.27_spmd} | conditional | flops 530063168 | bytes 14685557 | solution.py:241
  186.7 1.7 fusion.81
  189.4 1.6 fusion.73
  192.1 1.6 fusion.110
  193.6 2.6 collective-permute-start.3
  196.2 2.8 select_add_fusion.12
  199.0 2.8 select_add_fusion.13
  202.6 7.1 %conditional.13 = (f32[128,320]{0,1:T(8,128)S(1)}, f32[320,1280]{1,0:T(8,128)S(1)}, f32[1280,320]{0,1:T(8,128)S(1)}, f32[320]{0:T(512)S(1)}) conditional(s32[]{:T(128)} %convert_element_type.277, () %tuple.215, (pred[]{:T(512)}, bf16[4,128,320]{1,2,0:T(8,128)(2,1)S(1)}, s32[]{:T(128)}, bf16[128,320]{0,1:T(8,128)(2,1)S(1)}, ...), branch_computations={%region_23.23_spmd, %region_24.27_spmd} | conditional | flops 530063168 | bytes 14685557 | solution.py:241
  204.4 1.7 fusion.81
  207.1 1.6 fusion.73
  209.8 1.6 fusion.110
  212.7 2.8 select_add_fusion.12
  215.5 2.8 select_add_fusion.13
  219.1 7.1 %conditional.13 = (f32[128,320]{0,1:T(8,128)S(1)}, f32[320,1280]{1,0:T(8,128)S(1)}, f32[1280,320]{0,1:T(8,128)S(1)}, f32[320]{0:T(512)S(1)}) conditional(s32[]{:T(128)} %convert_element_type.277, () %tuple.215, (pred[]{:T(512)}, bf16[4,128,320]{1,2,0:T(8,128)(2,1)S(1)}, s32[]{:T(128)}, bf16[128,320]{0,1:T(8,128)(2,1)S(1)}, ...), branch_computations={%region_23.23_spmd, %region_24.27_spmd} | conditional | flops 530063168 | bytes 14685557 | solution.py:241
  220.9 1.7 fusion.81
  223.6 1.6 fusion.73
  226.2 1.6 fusion.110
  229.1 2.8 select_add_fusion.12
  231.9 2.8 select_add_fusion.13
  235.8 1.6 fusion.110
  237.4 8.2 %collective-permute-start.3 = (bf16[128,320]{0,1:T(8,128)(2,1)}, bf16[128,320]{0,1:T(8,128)(2,1)S(1)}, u32[]{:S(2)}, u32[]{:S(2)}) collective-permute-start(bf16[128,320]{0,1:T(8,128)(2,1)} %fusion.110), channel_id=1, source_target_pairs={{1,0},{3,2},{5,4},{7,6},{9,8},{11,10},{13,12},{15,14},{17,16},{19,... | collective-permute-start | bytes 245768 | tf_op jit(solution)/shard_map/while/body/eval_jaxpr/ppermute | solution.py:16
  245.5 2.8 select_add_fusion.12
  248.4 2.8 select_add_fusion.13
  251.2 102.2 %all-reduce.3 = (bf16[320,1280]{1,0:T(8,128)(2,1)}, bf16[1280,320]{0,1:T(8,128)(2,1)}, f32[1,320]{1,0:T(1,128)}, bf16[640,320]{0,1:T(8,128)(2,1)}, f32[1,640]{1,0:T(1,128)}) all-reduce(f32[320,1280]{1,0:T(8,128)} %get-tuple-element.1305, f32[1280,320]{0,1:T(8,128)} %get-tuple-element.1306, ...), channel_id=1, replica_groups=mesh['dp'=16,'pipe'=2] {'dp'}, use_global_device_ids=true, to_apply=%region_29.30 | all-reduce | flops 1024960 | bytes 6151680 | tf_op jit(solution)/shard_map/psum | solution.py:288
  (371 shorter events, 80.5 us)
Async XLA Ops:
  2.0 4.1 %copy-start.9 = (f32[4]{0:T(128)}, f32[4]{0:T(128)S(1)}, u32[]{:S(2)}) copy-start(f32[4]{0:T(128)S(1)} %get-tuple-element.1604) | copy-start | bytes 52
  2.0 4.1 %copy-start.11 = (f32[4]{0:T(128)}, f32[4]{0:T(128)S(1)}, u32[]{:S(2)}) copy-start(f32[4]{0:T(128)S(1)} %get-tuple-element.1605) | copy-start | bytes 52
  3.7 2.9 copy-start.5
  6.6 2.6 copy-start.6
  9.4 6.2 %collective-permute-start = (bf16[128,320]{0,1:T(8,128)(2,1)S(1)}, bf16[128,320]{0,1:T(8,128)(2,1)S(1)}, u32[]{:S(2)}, u32[]{:S(2)}) collective-permute-start(bf16[128,320]{0,1:T(8,128)(2,1)S(1)} %get-tuple-element.2172), channel_id=1, source_target_pairs={{0,1},{2,3},{4,5},{6,7},{8,9},{10,11},{12,13},{14,15},{16,17},{18,... | collective-permute-start | bytes 245768 | tf_op jit(solution)/shard_map/while/body/eval_jaxpr/ppermute | solution.py:16
  18.1 5.2 %collective-permute-start = (bf16[128,320]{0,1:T(8,128)(2,1)S(1)}, bf16[128,320]{0,1:T(8,128)(2,1)S(1)}, u32[]{:S(2)}, u32[]{:S(2)}) collective-permute-start(bf16[128,320]{0,1:T(8,128)(2,1)S(1)} %get-tuple-element.2172), channel_id=1, source_target_pairs={{0,1},{2,3},{4,5},{6,7},{8,9},{10,11},{12,13},{14,15},{16,17},{18,... | collective-permute-start | bytes 245768 | tf_op jit(solution)/shard_map/while/body/eval_jaxpr/ppermute | solution.py:16
  25.9 5.2 %collective-permute-start = (bf16[128,320]{0,1:T(8,128)(2,1)S(1)}, bf16[128,320]{0,1:T(8,128)(2,1)S(1)}, u32[]{:S(2)}, u32[]{:S(2)}) collective-permute-start(bf16[128,320]{0,1:T(8,128)(2,1)S(1)} %get-tuple-element.2172), channel_id=1, source_target_pairs={{0,1},{2,3},{4,5},{6,7},{8,9},{10,11},{12,13},{14,15},{16,17},{18,... | collective-permute-start | bytes 245768 | tf_op jit(solution)/shard_map/while/body/eval_jaxpr/ppermute | solution.py:16
  33.7 5.2 %collective-permute-start = (bf16[128,320]{0,1:T(8,128)(2,1)S(1)}, bf16[128,320]{0,1:T(8,128)(2,1)S(1)}, u32[]{:S(2)}, u32[]{:S(2)}) collective-permute-start(bf16[128,320]{0,1:T(8,128)(2,1)S(1)} %get-tuple-element.2172), channel_id=1, source_target_pairs={{0,1},{2,3},{4,5},{6,7},{8,9},{10,11},{12,13},{14,15},{16,17},{18,... | collective-permute-start | bytes 245768 | tf_op jit(solution)/shard_map/while/body/eval_jaxpr/ppermute | solution.py:16
  41.5 5.2 %collective-permute-start = (bf16[128,320]{0,1:T(8,128)(2,1)S(1)}, bf16[128,320]{0,1:T(8,128)(2,1)S(1)}, u32[]{:S(2)}, u32[]{:S(2)}) collective-permute-start(bf16[128,320]{0,1:T(8,128)(2,1)S(1)} %get-tuple-element.2172), channel_id=1, source_target_pairs={{0,1},{2,3},{4,5},{6,7},{8,9},{10,11},{12,13},{14,15},{16,17},{18,... | collective-permute-start | bytes 245768 | tf_op jit(solution)/shard_map/while/body/eval_jaxpr/ppermute | solution.py:16
  46.7 0.6 copy-start.8
  46.9 30.0 %copy-start.10 = (f32[4]{0:T(128)S(1)}, f32[4]{0:T(128)}, u32[]{:S(2)}) copy-start(f32[4]{0:T(128)} %copy-done.9) | copy-start | bytes 52
  46.9 30.0 %copy-start.12 = (f32[4]{0:T(128)S(1)}, f32[4]{0:T(128)}, u32[]{:S(2)}) copy-start(f32[4]{0:T(128)} %copy-done.11) | copy-start | bytes 52
  48.2 2.8 collective-permute-start.1
  51.8 5.9 %collective-permute-start.1 = (bf16[128,320]{0,1:T(8,128)(2,1)S(1)}, bf16[128,320]{0,1:T(8,128)(2,1)S(1)}, u32[]{:S(2)}, u32[]{:S(2)}) collective-permute-start(bf16[128,320]{0,1:T(8,128)(2,1)S(1)} %get-tuple-element.2173), channel_id=1, source_target_pairs={{1,0},{3,2},{5,4},{7,6},{9,8},{11,10},{13,12},{15,14},{17,16},{19,... | collective-permute-start | bytes 245768 | tf_op jit(solution)/shard_map/while/body/eval_jaxpr/ppermute | solution.py:16
  58.5 5.6 %collective-permute-start.1 = (bf16[128,320]{0,1:T(8,128)(2,1)S(1)}, bf16[128,320]{0,1:T(8,128)(2,1)S(1)}, u32[]{:S(2)}, u32[]{:S(2)}) collective-permute-start(bf16[128,320]{0,1:T(8,128)(2,1)S(1)} %get-tuple-element.2173), channel_id=1, source_target_pairs={{1,0},{3,2},{5,4},{7,6},{9,8},{11,10},{13,12},{15,14},{17,16},{19,... | collective-permute-start | bytes 245768 | tf_op jit(solution)/shard_map/while/body/eval_jaxpr/ppermute | solution.py:16
  64.9 5.5 %collective-permute-start.1 = (bf16[128,320]{0,1:T(8,128)(2,1)S(1)}, bf16[128,320]{0,1:T(8,128)(2,1)S(1)}, u32[]{:S(2)}, u32[]{:S(2)}) collective-permute-start(bf16[128,320]{0,1:T(8,128)(2,1)S(1)} %get-tuple-element.2173), channel_id=1, source_target_pairs={{1,0},{3,2},{5,4},{7,6},{9,8},{11,10},{13,12},{15,14},{17,16},{19,... | collective-permute-start | bytes 245768 | tf_op jit(solution)/shard_map/while/body/eval_jaxpr/ppermute | solution.py:16
  70.5 5.9 %collective-permute-start.1 = (bf16[128,320]{0,1:T(8,128)(2,1)S(1)}, bf16[128,320]{0,1:T(8,128)(2,1)S(1)}, u32[]{:S(2)}, u32[]{:S(2)}) collective-permute-start(bf16[128,320]{0,1:T(8,128)(2,1)S(1)} %get-tuple-element.2173), channel_id=1, source_target_pairs={{1,0},{3,2},{5,4},{7,6},{9,8},{11,10},{13,12},{15,14},{17,16},{19,... | collective-permute-start | bytes 245768 | tf_op jit(solution)/shard_map/while/body/eval_jaxpr/ppermute | solution.py:16
  76.4 56.2 %copy-start = (bf16[4,128,320]{1,2,0:T(8,128)(2,1)}, bf16[4,128,320]{1,2,0:T(8,128)(2,1)S(1)}, u32[]{:S(2)}) copy-start(bf16[4,128,320]{1,2,0:T(8,128)(2,1)S(1)} %get-tuple-element.2175) | copy-start | bytes 983044
  76.9 55.8 %copy-start.7 = (f32[1,640]{1,0:T(1,128)S(1)}, f32[1,640]{1,0:T(1,128)}, u32[]{:S(2)}) copy-start(f32[1,640]{1,0:T(1,128)} %param.33) | copy-start | bytes 7684
  132.8 5.4 %collective-permute-start.2 = (bf16[128,320]{1,0:T(8,128)(2,1)S(1)}, bf16[128,320]{1,0:T(8,128)(2,1)S(1)}, u32[]{:S(2)}, u32[]{:S(2)}) collective-permute-start(bf16[128,320]{1,0:T(8,128)(2,1)S(1)} %get-tuple-element.1924), channel_id=1, source_target_pairs={{0,1},{2,3},{4,5},{6,7},{8,9},{10,11},{12,13},{14,15},{16,17},{18,... | collective-permute-start | bytes 245768 | tf_op jit(solution)/shard_map/while/body/eval_jaxpr/ppermute | solution.py:16
  140.6 5.7 %collective-permute-start.2 = (bf16[128,320]{1,0:T(8,128)(2,1)S(1)}, bf16[128,320]{1,0:T(8,128)(2,1)S(1)}, u32[]{:S(2)}, u32[]{:S(2)}) collective-permute-start(bf16[128,320]{1,0:T(8,128)(2,1)S(1)} %get-tuple-element.1924), channel_id=1, source_target_pairs={{0,1},{2,3},{4,5},{6,7},{8,9},{10,11},{12,13},{14,15},{16,17},{18,... | collective-permute-start | bytes 245768 | tf_op jit(solution)/shard_map/while/body/eval_jaxpr/ppermute | solution.py:16
  148.7 5.7 %collective-permute-start.2 = (bf16[128,320]{1,0:T(8,128)(2,1)S(1)}, bf16[128,320]{1,0:T(8,128)(2,1)S(1)}, u32[]{:S(2)}, u32[]{:S(2)}) collective-permute-start(bf16[128,320]{1,0:T(8,128)(2,1)S(1)} %get-tuple-element.1924), channel_id=1, source_target_pairs={{0,1},{2,3},{4,5},{6,7},{8,9},{10,11},{12,13},{14,15},{16,17},{18,... | collective-permute-start | bytes 245768 | tf_op jit(solution)/shard_map/while/body/eval_jaxpr/ppermute | solution.py:16
  156.8 5.7 %collective-permute-start.2 = (bf16[128,320]{1,0:T(8,128)(2,1)S(1)}, bf16[128,320]{1,0:T(8,128)(2,1)S(1)}, u32[]{:S(2)}, u32[]{:S(2)}) collective-permute-start(bf16[128,320]{1,0:T(8,128)(2,1)S(1)} %get-tuple-element.1924), channel_id=1, source_target_pairs={{0,1},{2,3},{4,5},{6,7},{8,9},{10,11},{12,13},{14,15},{16,17},{18,... | collective-permute-start | bytes 245768 | tf_op jit(solution)/shard_map/while/body/eval_jaxpr/ppermute | solution.py:16
  164.9 5.7 %collective-permute-start.2 = (bf16[128,320]{1,0:T(8,128)(2,1)S(1)}, bf16[128,320]{1,0:T(8,128)(2,1)S(1)}, u32[]{:S(2)}, u32[]{:S(2)}) collective-permute-start(bf16[128,320]{1,0:T(8,128)(2,1)S(1)} %get-tuple-element.1924), channel_id=1, source_target_pairs={{0,1},{2,3},{4,5},{6,7},{8,9},{10,11},{12,13},{14,15},{16,17},{18,... | collective-permute-start | bytes 245768 | tf_op jit(solution)/shard_map/while/body/eval_jaxpr/ppermute | solution.py:16
  170.6 0.7 copy-start.2
  171.4 3.5 copy-start.4
  174.9 1.0 copy-start.1
  180.1 4.1 %collective-permute-start.3 = (bf16[128,320]{0,1:T(8,128)(2,1)}, bf16[128,320]{0,1:T(8,128)(2,1)S(1)}, u32[]{:S(2)}, u32[]{:S(2)}) collective-permute-start(bf16[128,320]{0,1:T(8,128)(2,1)} %fusion.110), channel_id=1, source_target_pairs={{1,0},{3,2},{5,4},{7,6},{9,8},{11,10},{13,12},{15,14},{17,16},{19,... | collective-permute-start | bytes 245768 | tf_op jit(solution)/shard_map/while/body/eval_jaxpr/ppermute | solution.py:16
  182.8 1.4 copy-start.3
  184.2 0.7 copy-start.2
  184.9 3.5 copy-start.4
  188.4 1.0 copy-start.1
  193.6 8.3 %collective-permute-start.3 = (bf16[128,320]{0,1:T(8,128)(2,1)}, bf16[128,320]{0,1:T(8,128)(2,1)S(1)}, u32[]{:S(2)}, u32[]{:S(2)}) collective-permute-start(bf16[128,320]{0,1:T(8,128)(2,1)} %fusion.110), channel_id=1, source_target_pairs={{1,0},{3,2},{5,4},{7,6},{9,8},{11,10},{13,12},{15,14},{17,16},{19,... | collective-permute-start | bytes 245768 | tf_op jit(solution)/shard_map/while/body/eval_jaxpr/ppermute | solution.py:16
  199.0 2.9 copy-start.3
  201.9 0.7 copy-start.2
  202.6 3.5 copy-start.4
  206.2 1.0 copy-start.1
  211.4 7.0 %collective-permute-start.3 = (bf16[128,320]{0,1:T(8,128)(2,1)}, bf16[128,320]{0,1:T(8,128)(2,1)S(1)}, u32[]{:S(2)}, u32[]{:S(2)}) collective-permute-start(bf16[128,320]{0,1:T(8,128)(2,1)} %fusion.110), channel_id=1, source_target_pairs={{1,0},{3,2},{5,4},{7,6},{9,8},{11,10},{13,12},{15,14},{17,16},{19,... | collective-permute-start | bytes 245768 | tf_op jit(solution)/shard_map/while/body/eval_jaxpr/ppermute | solution.py:16
  215.5 2.9 copy-start.3
  218.4 0.7 copy-start.2
  219.1 3.5 copy-start.4
  222.6 1.0 copy-start.1
  227.8 7.0 %collective-permute-start.3 = (bf16[128,320]{0,1:T(8,128)(2,1)}, bf16[128,320]{0,1:T(8,128)(2,1)S(1)}, u32[]{:S(2)}, u32[]{:S(2)}) collective-permute-start(bf16[128,320]{0,1:T(8,128)(2,1)} %fusion.110), channel_id=1, source_target_pairs={{1,0},{3,2},{5,4},{7,6},{9,8},{11,10},{13,12},{15,14},{17,16},{19,... | collective-permute-start | bytes 245768 | tf_op jit(solution)/shard_map/while/body/eval_jaxpr/ppermute | solution.py:16
  231.9 2.9 copy-start.3
  234.8 0.7 copy-start.2
  237.4 13.9 %collective-permute-start.3 = (bf16[128,320]{0,1:T(8,128)(2,1)}, bf16[128,320]{0,1:T(8,128)(2,1)S(1)}, u32[]{:S(2)}, u32[]{:S(2)}) collective-permute-start(bf16[128,320]{0,1:T(8,128)(2,1)} %fusion.110), channel_id=1, source_target_pairs={{1,0},{3,2},{5,4},{7,6},{9,8},{11,10},{13,12},{15,14},{17,16},{19,... | collective-permute-start | bytes 245768 | tf_op jit(solution)/shard_map/while/body/eval_jaxpr/ppermute | solution.py:16
  248.4 2.9 copy-start.3
